TPU v7x, 256 devices: a whole 4x4x8 slice. The times are simulated.
256 devices in a mesh: depth: 8 (over x_hi, y), row: 32 (over x_lo, z, core).
Axes of the slice: x: 4 (x_hi: 2, x_lo: 2; x = x_hi * 2 + x_lo), y: 4, z: 8, core: 2. Of those that a mesh axis runs over, the one named last changes fastest.
Arguments:
- index_volume: bfloat16 [8, 512, 2048], P('depth', 'row'), may hold values from -4 to 4
- angles: int32 [2], replicated, may hold values from 0 to 15
- offsets: int32 [8], P('depth'), may hold values from -4 to 4, as said below
- measured: bfloat16 [2, 512, 2048], P(None, 'row'), may hold values from 0 to 2
Outputs:
- gradient: float32 [8, 512, 2048], P('depth', 'row')
Inputs may be any that keep to these rules, and one draw needn't show every extreme that they name: `offsets`: each of -4 and 4 is taken by at least one slice.
All inputs are finite; a program needn't handle non-finite values.
Results may differ from a plain program's by a relative error of at most 0.0003.
Values may be sent and summed in bfloat16 or wider, within the bound.
A program may use at most 64 MiB of HBM per device.

v0:
```python
import math
import jax
import jax.numpy as jnp
from jax import lax
from jax.sharding import PartitionSpec as P

TILTS = 16
HALF = 10
SHIFT = 4
HALFCOL = 64
COLBLK = 128
PHASE_SCALE = 0.5
CHIRP_ROW = 1.3
CHIRP_COL = 1.7


def halo_rows(shard, axis, width):
    size, length = (lax.axis_size(axis), shard.shape[-2])
    up = [(i, i + 1) for i in range(size - 1)]
    down = [(j, i) for i, j in up]
    last = shard[..., length - width :, :]
    initial = shard[..., :width, :]
    before = lax.ppermute(last, axis, up)
    after = lax.ppermute(initial, axis, down)
    return jnp.concatenate([before, shard, after], axis=-2)


def kernel_values(distance, radius, chirp_rate):
    inside = jnp.abs(distance) <= radius
    phase_arg = chirp_rate / radius * distance * distance
    weight = 1.0 / math.sqrt(2 * radius + 1)
    real_part = jnp.where(inside, jnp.cos(phase_arg) * weight, 0.0)
    imag_part = jnp.where(inside, jnp.sin(phase_arg) * weight, 0.0)
    return (real_part, imag_part)


def row_band(offset, height, margin, conjugate):
    extent = (height, height + 2 * margin)
    target = lax.broadcasted_iota(jnp.int32, extent, 0)
    source = lax.broadcasted_iota(jnp.int32, extent, 1)
    offset_used = -offset if conjugate else offset
    distance = (source - target - margin - offset_used).astype(jnp.float32)
    real_part, imag_part = kernel_values(distance, HALF, CHIRP_ROW)
    return (real_part, -imag_part) if conjugate else (real_part, imag_part)


def column_band(conjugate, block_width):
    extent = (block_width + 2 * HALFCOL, block_width)
    source = lax.broadcasted_iota(jnp.int32, extent, 0)
    target = lax.broadcasted_iota(jnp.int32, extent, 1)
    distance = (source - target - HALFCOL).astype(jnp.float32)
    real_part, imag_part = kernel_values(distance, HALFCOL, CHIRP_COL)
    return (real_part, -imag_part) if conjugate else (real_part, imag_part)


def mix_rows(band, extended):

    def product(matrix, operand):
        return jnp.einsum("ij,jc->ic", matrix, operand, precision=lax.Precision.HIGHEST)

    real_part = product(band[0], extended[0]) - product(band[1], extended[1])
    imag_part = product(band[0], extended[1]) + product(band[1], extended[0])
    return jnp.stack([real_part, imag_part], axis=0)


def mix_columns(band, field):
    _, height, columns = field.shape
    blocks = columns // COLBLK
    padded = jnp.pad(field, ((0, 0), (0, 0), (HALFCOL, COLBLK - HALFCOL)))
    middle = padded[..., :columns].reshape(2, height, blocks, COLBLK)
    beyond = padded[..., COLBLK : columns + COLBLK].reshape(2, height, blocks, COLBLK)
    window = jnp.concatenate([middle, beyond], axis=3)

    def product(operand, matrix):
        return jnp.einsum("rbj,ji->rbi", operand, matrix, precision=lax.Precision.HIGH)

    real_part = product(window[0], band[0]) - product(window[1], band[1])
    imag_part = product(window[1], band[0]) + product(window[0], band[1])
    return jnp.stack([real_part, imag_part], axis=0).reshape(2, height, columns)


def rotate(field, cosine, sine):
    real_part = cosine * field[0] - sine * field[1]
    imag_part = cosine * field[1] + sine * field[0]
    return jnp.stack([real_part, imag_part], axis=0)


def plane_wave(angle, row_start, height, columns, total_rows, total_cols):
    across = angle - TILTS // 2
    along = jnp.mod(3 * angle, TILTS) - TILTS // 2
    row_index = row_start + lax.broadcasted_iota(jnp.int32, (height, columns), 0)
    col_index = lax.broadcasted_iota(jnp.int32, (height, columns), 1)
    period = total_cols * total_rows
    cycles_int = jnp.mod(across * col_index * total_rows + along * row_index * total_cols, period)
    phase_arg = 2.0 * math.pi / period * cycles_int.astype(jnp.float32)
    return jnp.stack([jnp.cos(phase_arg), jnp.sin(phase_arg)], axis=0)


def body(index_volume, angles, offsets, measured):
    sections = lax.axis_size("depth")
    section_no = lax.axis_index("depth")
    height = index_volume.shape[1]
    columns = index_volume.shape[2]
    margin = HALF + SHIFT
    row_start = lax.axis_index("row") * height
    total_rows = height * lax.axis_size("row")
    angle_count = angles.shape[0]
    angle_no = section_no % angle_count
    volume = lax.all_gather(index_volume, "depth", axis=0, tiled=True)
    shifts = lax.all_gather(offsets, "depth", axis=0, tiled=True)
    layers = volume.shape[0]
    intensity = lax.dynamic_index_in_dim(measured, angle_no, 0, keepdims=False).astype(jnp.float32)
    angle = lax.dynamic_index_in_dim(angles, angle_no, 0, keepdims=False)
    field = plane_wave(angle, row_start, height, columns, total_rows, columns)
    col_fwd = column_band(False, COLBLK)
    col_adj = column_band(True, COLBLK)
    phases = PHASE_SCALE * volume.astype(jnp.float32)
    cosines = jnp.cos(phases)
    sines = jnp.sin(phases)

    def forward_step(layer_no, carried):
        field, stored = carried
        transmitted = rotate(field, cosines[layer_no], sines[layer_no])
        stored = lax.dynamic_update_index_in_dim(stored, transmitted, layer_no, 0)
        extended = halo_rows(transmitted, "row", margin)
        band = row_band(shifts[layer_no], height, margin, False)
        return (mix_columns(col_fwd, mix_rows(band, extended)), stored)

    stored = jnp.zeros((layers,) + field.shape, jnp.float32)
    field, stored = lax.fori_loop(0, layers, forward_step, (field, stored))
    errors = field[0] * field[0] + field[1] * field[1] - intensity
    adjoint = 2.0 * errors[None] * field

    def backward_step(step, carried):
        adjoint, terms = carried
        layer_no = layers - 1 - step
        returned = mix_columns(col_adj, adjoint)
        extended = halo_rows(returned, "row", margin)
        band = row_band(shifts[layer_no], height, margin, True)
        returned = mix_rows(band, extended)
        transmitted = stored[layer_no]
        term = PHASE_SCALE * (transmitted[0] * returned[1] - transmitted[1] * returned[0])
        terms = lax.dynamic_update_index_in_dim(terms, term, layer_no, 0)
        return (rotate(returned, cosines[layer_no], -sines[layer_no]), terms)

    terms = jnp.zeros((layers, height, columns), jnp.float32)
    adjoint, terms = lax.fori_loop(0, layers, backward_step, (adjoint, terms))
    own = lax.dynamic_index_in_dim(terms, section_no, 0, keepdims=True)
    partner_slice = section_no ^ 1
    for_partner = lax.dynamic_index_in_dim(terms, partner_slice, 0, keepdims=True)
    pairs = [(i, i ^ 1) for i in range(sections)]
    received = lax.ppermute(for_partner, "depth", pairs)
    first = jnp.where(angle_no == 0, own, received)
    second = jnp.where(angle_no == 0, received, own)
    return first + second


def solution(mesh):
    in_specs = (P("depth", "row", None), P(), P("depth"), P(None, "row", None))
    out_specs = P("depth", "row", None)
    return jax.shard_map(body, mesh=mesh, in_specs=in_specs, out_specs=out_specs, check_vma=False)
```

profile of v0, /device:TPU:2, one launch (start us, length us, event | category | flops | bytes accessed | tf_op | source)
XLA Modules:
  0.0 368.7 jit_solution(4456685893062569715)
XLA Ops:
  5.0 12.8 %all-reduce.2 = s32[8]{0:T(128)S(1)} all-reduce(s32[8]{0:T(128)S(1)} %dynamic-update-slice), channel_id=1, replica_groups=mesh['depth'=8,'row'=32] {'depth'}, use_global_device_ids=true, to_apply=%add.2 | all-reduce | flops 8 | bytes 64
  17.7 35.1 %all_gather.7 = bf16[8,16,2048]{2,1,0:T(8,128)(2,1)S(1)} all-gather(bf16[1,16,2048]{2,1,0:T(8,128)(2,1)} %param.8), channel_id=1, replica_groups=mesh['depth'=8,'row'=32] {'depth'}, dimensions={0}, use_global_device_ids=true | all-gather | bytes 589824 | tf_op jit(solution)/shard_map/all_gather | solution.py:109
  52.8 3.7 %fusion.193 = (f32[8,16,2048]{2,1,0:T(8,128)S(1)}, f32[8,16,2048]{2,1,0:T(8,128)S(1)}) fusion(bf16[8,16,2048]{2,1,0:T(8,128)(2,1)S(1)} %all_gather.7), kind=kLoop, calls=%fused_computation.255 | loop fusion | flops 524288 | bytes 2621440 | tf_op jit(solution)/shard_map/sin | solution.py:119
  57.2 155.0 %while.38 = (s32[]{:T(128)}, f32[2,16,2048]{2,1,0:T(8,128)S(1)}, f32[8,2,16,2048]{3,2,1,0:T(8,128)}, s32[8]{0:T(128)S(1)}, f32[8,16,2048]{2,1,0:T(8,128)S(1)}, /*index=5*/f32[8,16,2048]{2,1,0:T(8,128)S(1)}, s32[]{:T(128)}) while((s32[]{:T(128)}, f32[2,16,2048]{2,1,0:T(8,128)S(1)}, f32[8,2,16,2048]{3,2,1,0:T(8,128)}, ...), condition=%wide.region_1.2_spmd.clone.clone, body=%wide.region_0.1_spmd.clone.clone.sunk | while | flops 273272320 | bytes 14237897 | solution.py:130
  57.3 1.9 collective-permute-start
  59.2 2.4 collective-permute-start.1
  63.1 8.9 %collective-permute-done.1 = f32[2,14,2048]{2,1,0:T(8,128)S(1)} collective-permute-done((f32[2,14,2048]{2,1,0:T(8,128)S(1)}, f32[2,14,2048]{2,1,0:T(8,128)S(1)}, u32[]{:S(2)}, u32[]{:S(2)}) %collective-permute-start.1) | collective-permute-done | bytes 229408 | tf_op jit(solution)/shard_map/while/body/eval_jaxpr/ppermute | solution.py:23
  79.3 1.9 collective-permute-start
  81.2 2.4 collective-permute-start.1
  85.1 5.9 %collective-permute-done.1 = f32[2,14,2048]{2,1,0:T(8,128)S(1)} collective-permute-done((f32[2,14,2048]{2,1,0:T(8,128)S(1)}, f32[2,14,2048]{2,1,0:T(8,128)S(1)}, u32[]{:S(2)}, u32[]{:S(2)}) %collective-permute-start.1) | collective-permute-done | bytes 229408 | tf_op jit(solution)/shard_map/while/body/eval_jaxpr/ppermute | solution.py:23
  100.2 2.4 collective-permute-start.1
  104.1 5.9 %collective-permute-done.1 = f32[2,14,2048]{2,1,0:T(8,128)S(1)} collective-permute-done((f32[2,14,2048]{2,1,0:T(8,128)S(1)}, f32[2,14,2048]{2,1,0:T(8,128)S(1)}, u32[]{:S(2)}, u32[]{:S(2)}) %collective-permute-start.1) | collective-permute-done | bytes 229408 | tf_op jit(solution)/shard_map/while/body/eval_jaxpr/ppermute | solution.py:23
  119.2 2.4 collective-permute-start.1
  123.1 5.9 %collective-permute-done.1 = f32[2,14,2048]{2,1,0:T(8,128)S(1)} collective-permute-done((f32[2,14,2048]{2,1,0:T(8,128)S(1)}, f32[2,14,2048]{2,1,0:T(8,128)S(1)}, u32[]{:S(2)}, u32[]{:S(2)}) %collective-permute-start.1) | collective-permute-done | bytes 229408 | tf_op jit(solution)/shard_map/while/body/eval_jaxpr/ppermute | solution.py:23
  138.2 2.4 collective-permute-start.1
  142.1 5.9 %collective-permute-done.1 = f32[2,14,2048]{2,1,0:T(8,128)S(1)} collective-permute-done((f32[2,14,2048]{2,1,0:T(8,128)S(1)}, f32[2,14,2048]{2,1,0:T(8,128)S(1)}, u32[]{:S(2)}, u32[]{:S(2)}) %collective-permute-start.1) | collective-permute-done | bytes 229408 | tf_op jit(solution)/shard_map/while/body/eval_jaxpr/ppermute | solution.py:23
  157.2 2.4 collective-permute-start.1
  161.1 5.9 %collective-permute-done.1 = f32[2,14,2048]{2,1,0:T(8,128)S(1)} collective-permute-done((f32[2,14,2048]{2,1,0:T(8,128)S(1)}, f32[2,14,2048]{2,1,0:T(8,128)S(1)}, u32[]{:S(2)}, u32[]{:S(2)}) %collective-permute-start.1) | collective-permute-done | bytes 229408 | tf_op jit(solution)/shard_map/while/body/eval_jaxpr/ppermute | solution.py:23
  176.2 2.4 collective-permute-start.1
  180.1 5.9 %collective-permute-done.1 = f32[2,14,2048]{2,1,0:T(8,128)S(1)} collective-permute-done((f32[2,14,2048]{2,1,0:T(8,128)S(1)}, f32[2,14,2048]{2,1,0:T(8,128)S(1)}, u32[]{:S(2)}, u32[]{:S(2)}) %collective-permute-start.1) | collective-permute-done | bytes 229408 | tf_op jit(solution)/shard_map/while/body/eval_jaxpr/ppermute | solution.py:23
  195.2 2.4 collective-permute-start.1
  199.1 5.9 %collective-permute-done.1 = f32[2,14,2048]{2,1,0:T(8,128)S(1)} collective-permute-done((f32[2,14,2048]{2,1,0:T(8,128)S(1)}, f32[2,14,2048]{2,1,0:T(8,128)S(1)}, u32[]{:S(2)}, u32[]{:S(2)}) %collective-permute-start.1) | collective-permute-done | bytes 229408 | tf_op jit(solution)/shard_map/while/body/eval_jaxpr/ppermute | solution.py:23
  213.3 147.8 %while.39 = (s32[]{:T(128)}, f32[2,16,2048]{2,1,0:T(8,128)S(1)}, f32[8,16,2048]{2,1,0:T(8,128)}, f32[8,16,2048]{2,1,0:T(8,128)S(1)}, s32[8]{0:T(128)S(1)}, /*ind...) while((s32[]{:T(128)}, f32[2,16,2048]{2,1,0:T(8,128)S(1)}, ...), condition=%wide.region_3.4_spmd.clone.clone, body=%wide.region_2.3_spmd.clone.clone.sunk | while | flops 272724864 | bytes 14156587 | solution.py:147
  218.8 2.4 collective-permute-start.3
  222.6 5.9 %collective-permute-done.3 = f32[2,14,2048]{2,1,0:T(8,128)S(1)} collective-permute-done((f32[2,14,2048]{2,1,0:T(8,128)S(1)}, f32[2,14,2048]{2,1,0:T(8,128)S(1)}, u32[]{:S(2)}, u32[]{:S(2)}) %collective-permute-start.3) | collective-permute-done | bytes 229408 | tf_op jit(solution)/shard_map/while/body/eval_jaxpr/ppermute | solution.py:23
  229.7 2.0 fusion.248
  237.2 2.4 collective-permute-start.3
  241.1 5.9 %collective-permute-done.3 = f32[2,14,2048]{2,1,0:T(8,128)S(1)} collective-permute-done((f32[2,14,2048]{2,1,0:T(8,128)S(1)}, f32[2,14,2048]{2,1,0:T(8,128)S(1)}, u32[]{:S(2)}, u32[]{:S(2)}) %collective-permute-start.3) | collective-permute-done | bytes 229408 | tf_op jit(solution)/shard_map/while/body/eval_jaxpr/ppermute | solution.py:23
  248.2 2.0 fusion.248
  255.7 2.4 collective-permute-start.3
  259.6 5.9 %collective-permute-done.3 = f32[2,14,2048]{2,1,0:T(8,128)S(1)} collective-permute-done((f32[2,14,2048]{2,1,0:T(8,128)S(1)}, f32[2,14,2048]{2,1,0:T(8,128)S(1)}, u32[]{:S(2)}, u32[]{:S(2)}) %collective-permute-start.3) | collective-permute-done | bytes 229408 | tf_op jit(solution)/shard_map/while/body/eval_jaxpr/ppermute | solution.py:23
  266.7 2.0 fusion.248
  274.2 2.4 collective-permute-start.3
  278.1 5.9 %collective-permute-done.3 = f32[2,14,2048]{2,1,0:T(8,128)S(1)} collective-permute-done((f32[2,14,2048]{2,1,0:T(8,128)S(1)}, f32[2,14,2048]{2,1,0:T(8,128)S(1)}, u32[]{:S(2)}, u32[]{:S(2)}) %collective-permute-start.3) | collective-permute-done | bytes 229408 | tf_op jit(solution)/shard_map/while/body/eval_jaxpr/ppermute | solution.py:23
  285.2 2.0 fusion.248
  292.7 2.4 collective-permute-start.3
  296.5 5.9 %collective-permute-done.3 = f32[2,14,2048]{2,1,0:T(8,128)S(1)} collective-permute-done((f32[2,14,2048]{2,1,0:T(8,128)S(1)}, f32[2,14,2048]{2,1,0:T(8,128)S(1)}, u32[]{:S(2)}, u32[]{:S(2)}) %collective-permute-start.3) | collective-permute-done | bytes 229408 | tf_op jit(solution)/shard_map/while/body/eval_jaxpr/ppermute | solution.py:23
  303.6 2.0 fusion.248
  311.2 2.4 collective-permute-start.3
  315.0 5.9 %collective-permute-done.3 = f32[2,14,2048]{2,1,0:T(8,128)S(1)} collective-permute-done((f32[2,14,2048]{2,1,0:T(8,128)S(1)}, f32[2,14,2048]{2,1,0:T(8,128)S(1)}, u32[]{:S(2)}, u32[]{:S(2)}) %collective-permute-start.3) | collective-permute-done | bytes 229408 | tf_op jit(solution)/shard_map/while/body/eval_jaxpr/ppermute | solution.py:23
  322.1 2.0 fusion.248
  329.6 2.4 collective-permute-start.3
  333.5 5.9 %collective-permute-done.3 = f32[2,14,2048]{2,1,0:T(8,128)S(1)} collective-permute-done((f32[2,14,2048]{2,1,0:T(8,128)S(1)}, f32[2,14,2048]{2,1,0:T(8,128)S(1)}, u32[]{:S(2)}, u32[]{:S(2)}) %collective-permute-start.3) | collective-permute-done | bytes 229408 | tf_op jit(solution)/shard_map/while/body/eval_jaxpr/ppermute | solution.py:23
  340.6 2.0 fusion.248
  348.1 2.4 collective-permute-start.3
  352.0 5.9 %collective-permute-done.3 = f32[2,14,2048]{2,1,0:T(8,128)S(1)} collective-permute-done((f32[2,14,2048]{2,1,0:T(8,128)S(1)}, f32[2,14,2048]{2,1,0:T(8,128)S(1)}, u32[]{:S(2)}, u32[]{:S(2)}) %collective-permute-start.3) | collective-permute-done | bytes 229408 | tf_op jit(solution)/shard_map/while/body/eval_jaxpr/ppermute | solution.py:23
  359.0 2.0 fusion.248
  362.1 4.9 %collective-permute-done.4 = f32[1,16,2048]{2,1,0:T(8,128)S(1)} collective-permute-done((f32[1,16,2048]{2,1,0:T(8,128)S(1)}, f32[1,16,2048]{2,1,0:T(8,128)S(1)}, u32[]{:S(2)}, u32[]{:S(2)}) %collective-permute-start.4) | collective-permute-done | bytes 131104 | tf_op jit(solution)/shard_map/ppermute | solution.py:152
  (391 shorter events, 146.2 us)
Async XLA Ops:
  57.1 155.0 %copy-start = (bf16[2,16,2048]{2,1,0:T(8,128)(2,1)S(1)}, bf16[2,16,2048]{2,1,0:T(8,128)(2,1)}, u32[]{:S(2)}) copy-start(bf16[2,16,2048]{2,1,0:T(8,128)(2,1)} %param.11) | copy-start | bytes 393220
  57.3 5.8 %collective-permute-start = (f32[2,14,2048]{2,1,0:T(8,128)S(1)}, f32[2,14,2048]{2,1,0:T(8,128)S(1)}, u32[]{:S(2)}, u32[]{:S(2)}) collective-permute-start(f32[2,14,2048]{2,1,0:T(8,128)S(1)} %get-tuple-element.655), channel_id=1, source_target_pairs={{1,0},{2,1},{3,2},{4,3},{5,4},{6,5},{7,6},{8,7},{9,8},{10,9},{11,1... | collective-permute-start | bytes 688136 | tf_op jit(solution)/shard_map/while/body/eval_jaxpr/ppermute | solution.py:24
  59.2 12.8 %collective-permute-start.1 = (f32[2,14,2048]{2,1,0:T(8,128)S(1)}, f32[2,14,2048]{2,1,0:T(8,128)S(1)}, u32[]{:S(2)}, u32[]{:S(2)}) collective-permute-start(f32[2,14,2048]{2,1,0:T(8,128)S(1)} %get-tuple-element.656), channel_id=1, source_target_pairs={{0,1},{1,2},{2,3},{3,4},{4,5},{5,6},{6,7},{7,8},{8,9},{9,10},{10,1... | collective-permute-start | bytes 688136 | tf_op jit(solution)/shard_map/while/body/eval_jaxpr/ppermute | solution.py:23
  79.3 5.8 %collective-permute-start = (f32[2,14,2048]{2,1,0:T(8,128)S(1)}, f32[2,14,2048]{2,1,0:T(8,128)S(1)}, u32[]{:S(2)}, u32[]{:S(2)}) collective-permute-start(f32[2,14,2048]{2,1,0:T(8,128)S(1)} %get-tuple-element.655), channel_id=1, source_target_pairs={{1,0},{2,1},{3,2},{4,3},{5,4},{6,5},{7,6},{8,7},{9,8},{10,9},{11,1... | collective-permute-start | bytes 688136 | tf_op jit(solution)/shard_map/while/body/eval_jaxpr/ppermute | solution.py:24
  81.2 9.8 %collective-permute-start.1 = (f32[2,14,2048]{2,1,0:T(8,128)S(1)}, f32[2,14,2048]{2,1,0:T(8,128)S(1)}, u32[]{:S(2)}, u32[]{:S(2)}) collective-permute-start(f32[2,14,2048]{2,1,0:T(8,128)S(1)} %get-tuple-element.656), channel_id=1, source_target_pairs={{0,1},{1,2},{2,3},{3,4},{4,5},{5,6},{6,7},{7,8},{8,9},{9,10},{10,1... | collective-permute-start | bytes 688136 | tf_op jit(solution)/shard_map/while/body/eval_jaxpr/ppermute | solution.py:23
  98.3 5.8 %collective-permute-start = (f32[2,14,2048]{2,1,0:T(8,128)S(1)}, f32[2,14,2048]{2,1,0:T(8,128)S(1)}, u32[]{:S(2)}, u32[]{:S(2)}) collective-permute-start(f32[2,14,2048]{2,1,0:T(8,128)S(1)} %get-tuple-element.655), channel_id=1, source_target_pairs={{1,0},{2,1},{3,2},{4,3},{5,4},{6,5},{7,6},{8,7},{9,8},{10,9},{11,1... | collective-permute-start | bytes 688136 | tf_op jit(solution)/shard_map/while/body/eval_jaxpr/ppermute | solution.py:24
  100.2 9.8 %collective-permute-start.1 = (f32[2,14,2048]{2,1,0:T(8,128)S(1)}, f32[2,14,2048]{2,1,0:T(8,128)S(1)}, u32[]{:S(2)}, u32[]{:S(2)}) collective-permute-start(f32[2,14,2048]{2,1,0:T(8,128)S(1)} %get-tuple-element.656), channel_id=1, source_target_pairs={{0,1},{1,2},{2,3},{3,4},{4,5},{5,6},{6,7},{7,8},{8,9},{9,10},{10,1... | collective-permute-start | bytes 688136 | tf_op jit(solution)/shard_map/while/body/eval_jaxpr/ppermute | solution.py:23
  117.3 5.8 %collective-permute-start = (f32[2,14,2048]{2,1,0:T(8,128)S(1)}, f32[2,14,2048]{2,1,0:T(8,128)S(1)}, u32[]{:S(2)}, u32[]{:S(2)}) collective-permute-start(f32[2,14,2048]{2,1,0:T(8,128)S(1)} %get-tuple-element.655), channel_id=1, source_target_pairs={{1,0},{2,1},{3,2},{4,3},{5,4},{6,5},{7,6},{8,7},{9,8},{10,9},{11,1... | collective-permute-start | bytes 688136 | tf_op jit(solution)/shard_map/while/body/eval_jaxpr/ppermute | solution.py:24
  119.2 9.8 %collective-permute-start.1 = (f32[2,14,2048]{2,1,0:T(8,128)S(1)}, f32[2,14,2048]{2,1,0:T(8,128)S(1)}, u32[]{:S(2)}, u32[]{:S(2)}) collective-permute-start(f32[2,14,2048]{2,1,0:T(8,128)S(1)} %get-tuple-element.656), channel_id=1, source_target_pairs={{0,1},{1,2},{2,3},{3,4},{4,5},{5,6},{6,7},{7,8},{8,9},{9,10},{10,1... | collective-permute-start | bytes 688136 | tf_op jit(solution)/shard_map/while/body/eval_jaxpr/ppermute | solution.py:23
  136.3 5.8 %collective-permute-start = (f32[2,14,2048]{2,1,0:T(8,128)S(1)}, f32[2,14,2048]{2,1,0:T(8,128)S(1)}, u32[]{:S(2)}, u32[]{:S(2)}) collective-permute-start(f32[2,14,2048]{2,1,0:T(8,128)S(1)} %get-tuple-element.655), channel_id=1, source_target_pairs={{1,0},{2,1},{3,2},{4,3},{5,4},{6,5},{7,6},{8,7},{9,8},{10,9},{11,1... | collective-permute-start | bytes 688136 | tf_op jit(solution)/shard_map/while/body/eval_jaxpr/ppermute | solution.py:24
  138.2 9.8 %collective-permute-start.1 = (f32[2,14,2048]{2,1,0:T(8,128)S(1)}, f32[2,14,2048]{2,1,0:T(8,128)S(1)}, u32[]{:S(2)}, u32[]{:S(2)}) collective-permute-start(f32[2,14,2048]{2,1,0:T(8,128)S(1)} %get-tuple-element.656), channel_id=1, source_target_pairs={{0,1},{1,2},{2,3},{3,4},{4,5},{5,6},{6,7},{7,8},{8,9},{9,10},{10,1... | collective-permute-start | bytes 688136 | tf_op jit(solution)/shard_map/while/body/eval_jaxpr/ppermute | solution.py:23
  155.3 5.8 %collective-permute-start = (f32[2,14,2048]{2,1,0:T(8,128)S(1)}, f32[2,14,2048]{2,1,0:T(8,128)S(1)}, u32[]{:S(2)}, u32[]{:S(2)}) collective-permute-start(f32[2,14,2048]{2,1,0:T(8,128)S(1)} %get-tuple-element.655), channel_id=1, source_target_pairs={{1,0},{2,1},{3,2},{4,3},{5,4},{6,5},{7,6},{8,7},{9,8},{10,9},{11,1... | collective-permute-start | bytes 688136 | tf_op jit(solution)/shard_map/while/body/eval_jaxpr/ppermute | solution.py:24
  157.2 9.8 %collective-permute-start.1 = (f32[2,14,2048]{2,1,0:T(8,128)S(1)}, f32[2,14,2048]{2,1,0:T(8,128)S(1)}, u32[]{:S(2)}, u32[]{:S(2)}) collective-permute-start(f32[2,14,2048]{2,1,0:T(8,128)S(1)} %get-tuple-element.656), channel_id=1, source_target_pairs={{0,1},{1,2},{2,3},{3,4},{4,5},{5,6},{6,7},{7,8},{8,9},{9,10},{10,1... | collective-permute-start | bytes 688136 | tf_op jit(solution)/shard_map/while/body/eval_jaxpr/ppermute | solution.py:23
  174.3 5.8 %collective-permute-start = (f32[2,14,2048]{2,1,0:T(8,128)S(1)}, f32[2,14,2048]{2,1,0:T(8,128)S(1)}, u32[]{:S(2)}, u32[]{:S(2)}) collective-permute-start(f32[2,14,2048]{2,1,0:T(8,128)S(1)} %get-tuple-element.655), channel_id=1, source_target_pairs={{1,0},{2,1},{3,2},{4,3},{5,4},{6,5},{7,6},{8,7},{9,8},{10,9},{11,1... | collective-permute-start | bytes 688136 | tf_op jit(solution)/shard_map/while/body/eval_jaxpr/ppermute | solution.py:24
  176.2 9.8 %collective-permute-start.1 = (f32[2,14,2048]{2,1,0:T(8,128)S(1)}, f32[2,14,2048]{2,1,0:T(8,128)S(1)}, u32[]{:S(2)}, u32[]{:S(2)}) collective-permute-start(f32[2,14,2048]{2,1,0:T(8,128)S(1)} %get-tuple-element.656), channel_id=1, source_target_pairs={{0,1},{1,2},{2,3},{3,4},{4,5},{5,6},{6,7},{7,8},{8,9},{9,10},{10,1... | collective-permute-start | bytes 688136 | tf_op jit(solution)/shard_map/while/body/eval_jaxpr/ppermute | solution.py:23
  193.3 5.8 %collective-permute-start = (f32[2,14,2048]{2,1,0:T(8,128)S(1)}, f32[2,14,2048]{2,1,0:T(8,128)S(1)}, u32[]{:S(2)}, u32[]{:S(2)}) collective-permute-start(f32[2,14,2048]{2,1,0:T(8,128)S(1)} %get-tuple-element.655), channel_id=1, source_target_pairs={{1,0},{2,1},{3,2},{4,3},{5,4},{6,5},{7,6},{8,7},{9,8},{10,9},{11,1... | collective-permute-start | bytes 688136 | tf_op jit(solution)/shard_map/while/body/eval_jaxpr/ppermute | solution.py:24
  195.2 9.8 %collective-permute-start.1 = (f32[2,14,2048]{2,1,0:T(8,128)S(1)}, f32[2,14,2048]{2,1,0:T(8,128)S(1)}, u32[]{:S(2)}, u32[]{:S(2)}) collective-permute-start(f32[2,14,2048]{2,1,0:T(8,128)S(1)} %get-tuple-element.656), channel_id=1, source_target_pairs={{0,1},{1,2},{2,3},{3,4},{4,5},{5,6},{6,7},{7,8},{8,9},{9,10},{10,1... | collective-permute-start | bytes 688136 | tf_op jit(solution)/shard_map/while/body/eval_jaxpr/ppermute | solution.py:23
  216.8 5.8 %collective-permute-start.2 = (f32[2,14,2048]{2,1,0:T(8,128)S(1)}, f32[2,14,2048]{2,1,0:T(8,128)S(1)}, u32[]{:S(2)}, u32[]{:S(2)}) collective-permute-start(f32[2,14,2048]{2,1,0:T(8,128)S(1)} %get-tuple-element.668), channel_id=1, source_target_pairs={{1,0},{2,1},{3,2},{4,3},{5,4},{6,5},{7,6},{8,7},{9,8},{10,9},{11,1... | collective-permute-start | bytes 688136 | tf_op jit(solution)/shard_map/while/body/eval_jaxpr/ppermute | solution.py:24
  218.8 9.8 %collective-permute-start.3 = (f32[2,14,2048]{2,1,0:T(8,128)S(1)}, f32[2,14,2048]{2,1,0:T(8,128)S(1)}, u32[]{:S(2)}, u32[]{:S(2)}) collective-permute-start(f32[2,14,2048]{2,1,0:T(8,128)S(1)} %get-tuple-element.669), channel_id=1, source_target_pairs={{0,1},{1,2},{2,3},{3,4},{4,5},{5,6},{6,7},{7,8},{8,9},{9,10},{10,1... | collective-permute-start | bytes 688136 | tf_op jit(solution)/shard_map/while/body/eval_jaxpr/ppermute | solution.py:23
  235.3 5.8 %collective-permute-start.2 = (f32[2,14,2048]{2,1,0:T(8,128)S(1)}, f32[2,14,2048]{2,1,0:T(8,128)S(1)}, u32[]{:S(2)}, u32[]{:S(2)}) collective-permute-start(f32[2,14,2048]{2,1,0:T(8,128)S(1)} %get-tuple-element.668), channel_id=1, source_target_pairs={{1,0},{2,1},{3,2},{4,3},{5,4},{6,5},{7,6},{8,7},{9,8},{10,9},{11,1... | collective-permute-start | bytes 688136 | tf_op jit(solution)/shard_map/while/body/eval_jaxpr/ppermute | solution.py:24
  237.2 9.8 %collective-permute-start.3 = (f32[2,14,2048]{2,1,0:T(8,128)S(1)}, f32[2,14,2048]{2,1,0:T(8,128)S(1)}, u32[]{:S(2)}, u32[]{:S(2)}) collective-permute-start(f32[2,14,2048]{2,1,0:T(8,128)S(1)} %get-tuple-element.669), channel_id=1, source_target_pairs={{0,1},{1,2},{2,3},{3,4},{4,5},{5,6},{6,7},{7,8},{8,9},{9,10},{10,1... | collective-permute-start | bytes 688136 | tf_op jit(solution)/shard_map/while/body/eval_jaxpr/ppermute | solution.py:23
  253.8 5.8 %collective-permute-start.2 = (f32[2,14,2048]{2,1,0:T(8,128)S(1)}, f32[2,14,2048]{2,1,0:T(8,128)S(1)}, u32[]{:S(2)}, u32[]{:S(2)}) collective-permute-start(f32[2,14,2048]{2,1,0:T(8,128)S(1)} %get-tuple-element.668), channel_id=1, source_target_pairs={{1,0},{2,1},{3,2},{4,3},{5,4},{6,5},{7,6},{8,7},{9,8},{10,9},{11,1... | collective-permute-start | bytes 688136 | tf_op jit(solution)/shard_map/while/body/eval_jaxpr/ppermute | solution.py:24
  255.7 9.8 %collective-permute-start.3 = (f32[2,14,2048]{2,1,0:T(8,128)S(1)}, f32[2,14,2048]{2,1,0:T(8,128)S(1)}, u32[]{:S(2)}, u32[]{:S(2)}) collective-permute-start(f32[2,14,2048]{2,1,0:T(8,128)S(1)} %get-tuple-element.669), channel_id=1, source_target_pairs={{0,1},{1,2},{2,3},{3,4},{4,5},{5,6},{6,7},{7,8},{8,9},{9,10},{10,1... | collective-permute-start | bytes 688136 | tf_op jit(solution)/shard_map/while/body/eval_jaxpr/ppermute | solution.py:23
  272.3 5.8 %collective-permute-start.2 = (f32[2,14,2048]{2,1,0:T(8,128)S(1)}, f32[2,14,2048]{2,1,0:T(8,128)S(1)}, u32[]{:S(2)}, u32[]{:S(2)}) collective-permute-start(f32[2,14,2048]{2,1,0:T(8,128)S(1)} %get-tuple-element.668), channel_id=1, source_target_pairs={{1,0},{2,1},{3,2},{4,3},{5,4},{6,5},{7,6},{8,7},{9,8},{10,9},{11,1... | collective-permute-start | bytes 688136 | tf_op jit(solution)/shard_map/while/body/eval_jaxpr/ppermute | solution.py:24
  274.2 9.8 %collective-permute-start.3 = (f32[2,14,2048]{2,1,0:T(8,128)S(1)}, f32[2,14,2048]{2,1,0:T(8,128)S(1)}, u32[]{:S(2)}, u32[]{:S(2)}) collective-permute-start(f32[2,14,2048]{2,1,0:T(8,128)S(1)} %get-tuple-element.669), channel_id=1, source_target_pairs={{0,1},{1,2},{2,3},{3,4},{4,5},{5,6},{6,7},{7,8},{8,9},{9,10},{10,1... | collective-permute-start | bytes 688136 | tf_op jit(solution)/shard_map/while/body/eval_jaxpr/ppermute | solution.py:23
  290.7 5.8 %collective-permute-start.2 = (f32[2,14,2048]{2,1,0:T(8,128)S(1)}, f32[2,14,2048]{2,1,0:T(8,128)S(1)}, u32[]{:S(2)}, u32[]{:S(2)}) collective-permute-start(f32[2,14,2048]{2,1,0:T(8,128)S(1)} %get-tuple-element.668), channel_id=1, source_target_pairs={{1,0},{2,1},{3,2},{4,3},{5,4},{6,5},{7,6},{8,7},{9,8},{10,9},{11,1... | collective-permute-start | bytes 688136 | tf_op jit(solution)/shard_map/while/body/eval_jaxpr/ppermute | solution.py:24
  292.7 9.8 %collective-permute-start.3 = (f32[2,14,2048]{2,1,0:T(8,128)S(1)}, f32[2,14,2048]{2,1,0:T(8,128)S(1)}, u32[]{:S(2)}, u32[]{:S(2)}) collective-permute-start(f32[2,14,2048]{2,1,0:T(8,128)S(1)} %get-tuple-element.669), channel_id=1, source_target_pairs={{0,1},{1,2},{2,3},{3,4},{4,5},{5,6},{6,7},{7,8},{8,9},{9,10},{10,1... | collective-permute-start | bytes 688136 | tf_op jit(solution)/shard_map/while/body/eval_jaxpr/ppermute | solution.py:23
  309.2 5.8 %collective-permute-start.2 = (f32[2,14,2048]{2,1,0:T(8,128)S(1)}, f32[2,14,2048]{2,1,0:T(8,128)S(1)}, u32[]{:S(2)}, u32[]{:S(2)}) collective-permute-start(f32[2,14,2048]{2,1,0:T(8,128)S(1)} %get-tuple-element.668), channel_id=1, source_target_pairs={{1,0},{2,1},{3,2},{4,3},{5,4},{6,5},{7,6},{8,7},{9,8},{10,9},{11,1... | collective-permute-start | bytes 688136 | tf_op jit(solution)/shard_map/while/body/eval_jaxpr/ppermute | solution.py:24
  311.2 9.8 %collective-permute-start.3 = (f32[2,14,2048]{2,1,0:T(8,128)S(1)}, f32[2,14,2048]{2,1,0:T(8,128)S(1)}, u32[]{:S(2)}, u32[]{:S(2)}) collective-permute-start(f32[2,14,2048]{2,1,0:T(8,128)S(1)} %get-tuple-element.669), channel_id=1, source_target_pairs={{0,1},{1,2},{2,3},{3,4},{4,5},{5,6},{6,7},{7,8},{8,9},{9,10},{10,1... | collective-permute-start | bytes 688136 | tf_op jit(solution)/shard_map/while/body/eval_jaxpr/ppermute | solution.py:23
  327.7 5.8 %collective-permute-start.2 = (f32[2,14,2048]{2,1,0:T(8,128)S(1)}, f32[2,14,2048]{2,1,0:T(8,128)S(1)}, u32[]{:S(2)}, u32[]{:S(2)}) collective-permute-start(f32[2,14,2048]{2,1,0:T(8,128)S(1)} %get-tuple-element.668), channel_id=1, source_target_pairs={{1,0},{2,1},{3,2},{4,3},{5,4},{6,5},{7,6},{8,7},{9,8},{10,9},{11,1... | collective-permute-start | bytes 688136 | tf_op jit(solution)/shard_map/while/body/eval_jaxpr/ppermute | solution.py:24
  329.6 9.8 %collective-permute-start.3 = (f32[2,14,2048]{2,1,0:T(8,128)S(1)}, f32[2,14,2048]{2,1,0:T(8,128)S(1)}, u32[]{:S(2)}, u32[]{:S(2)}) collective-permute-start(f32[2,14,2048]{2,1,0:T(8,128)S(1)} %get-tuple-element.669), channel_id=1, source_target_pairs={{0,1},{1,2},{2,3},{3,4},{4,5},{5,6},{6,7},{7,8},{8,9},{9,10},{10,1... | collective-permute-start | bytes 688136 | tf_op jit(solution)/shard_map/while/body/eval_jaxpr/ppermute | solution.py:23
  346.2 5.8 %collective-permute-start.2 = (f32[2,14,2048]{2,1,0:T(8,128)S(1)}, f32[2,14,2048]{2,1,0:T(8,128)S(1)}, u32[]{:S(2)}, u32[]{:S(2)}) collective-permute-start(f32[2,14,2048]{2,1,0:T(8,128)S(1)} %get-tuple-element.668), channel_id=1, source_target_pairs={{1,0},{2,1},{3,2},{4,3},{5,4},{6,5},{7,6},{8,7},{9,8},{10,9},{11,1... | collective-permute-start | bytes 688136 | tf_op jit(solution)/shard_map/while/body/eval_jaxpr/ppermute | solution.py:24
  348.1 9.8 %collective-permute-start.3 = (f32[2,14,2048]{2,1,0:T(8,128)S(1)}, f32[2,14,2048]{2,1,0:T(8,128)S(1)}, u32[]{:S(2)}, u32[]{:S(2)}) collective-permute-start(f32[2,14,2048]{2,1,0:T(8,128)S(1)} %get-tuple-element.669), channel_id=1, source_target_pairs={{0,1},{1,2},{2,3},{3,4},{4,5},{5,6},{6,7},{7,8},{8,9},{9,10},{10,1... | collective-permute-start | bytes 688136 | tf_op jit(solution)/shard_map/while/body/eval_jaxpr/ppermute | solution.py:23
  362.0 5.1 %collective-permute-start.4 = (f32[1,16,2048]{2,1,0:T(8,128)S(1)}, f32[1,16,2048]{2,1,0:T(8,128)S(1)}, u32[]{:S(2)}, u32[]{:S(2)}) collective-permute-start(f32[1,16,2048]{2,1,0:T(8,128)S(1)} %constant_dynamic-slice_fusion), channel_id=1, source_target_pairs={{0,32},{32,0},{64,96},{96,64},{128,160},{160,128},{192,224},{224,1... | collective-permute-start | bytes 393224 | tf_op jit(solution)/shard_map/ppermute | solution.py:152
where the time goes:
time: 370 us; the launch traced here: 369 us
  waiting for transfers between devices  105 us (28%)
  matrix products  100 us (27%)
  starting transfers between devices  69.3 us (19%)
  blocking collectives  47.8 us (13%)
  local copies, waits for them, and re-layouts  20.5 us (6%)
  other arithmetic  15.5 us (4%)
  loops' own time  7.87 us (2%)
    ppermute x16, waiting for transfers between devices, halo_rows(): before = lax.ppermute(last, axis, up)  97.9 us
    dot_general x64, matrix products, product(): jnp.einsum('ij,jc->ic', matrix, operand, precision=lax.Precision.HIGHEST)  53.2 us
    dot_general x64, matrix products, product(): jnp.einsum('rbj,ji->rbi', operand, matrix, precision=lax.Precision.HIGH)  47.2 us
    ppermute x16, starting transfers between devices, halo_rows(): before = lax.ppermute(last, axis, up)  38.5 us
    all_gather x1, blocking collectives, body(): volume = lax.all_gather(index_volume, 'depth', axis=0, tiled=True)  35.1 us
    ppermute x16, starting transfers between devices, halo_rows(): after = lax.ppermute(initial, axis, down)  30.7 us
    unnamed x1, blocking collectives  12.8 us
  transfers between devices with their start and end apart: 33, of which 33 were waited for; matrix products, arithmetic and copies ran while one was open for 4% of the time, Pallas kernels for 0%

commit v1 on v0

--- a/solution.py
+++ b/solution.py
@@ -106,7 +106,9 @@
     total_rows = height * lax.axis_size("row")
     angle_count = angles.shape[0]
     angle_no = section_no % angle_count
-    volume = lax.all_gather(index_volume, "depth", axis=0, tiled=True)
+    volume = jnp.concatenate(
+        lax.all_to_all(jnp.stack([index_volume] * lax.axis_size("depth")), "depth", 0, 0), axis=0
+    )
     shifts = lax.all_gather(offsets, "depth", axis=0, tiled=True)
     layers = volume.shape[0]
     intensity = lax.dynamic_index_in_dim(measured, angle_no, 0, keepdims=False).astype(jnp.float32)

time: 370 us -> 347 us (0.938)
  blocking collectives: 47.8 us -> 13.9 us
  starting transfers between devices: 69.3 us -> 78.1 us
    all_gather x1 -> x0, blocking collectives: 35.1 us -> none  [body(): volume = lax.all_gather(index_volume, 'depth', axis=0, tiled=True)]
    all_to_all x0 -> x1, starting transfers between devices: none -> 6.03 us  [body(): lax.all_to_all(jnp.stack([index_volume] * lax.axis_size('depth')), 'depth...]
  transfers between devices with their start and end apart: 33 -> 34, of which waited for: 33 -> 33; matrix products, arithmetic and copies ran while one was open for 4% -> 6% of each run, Pallas kernels for 0% -> 0%
where the time goes in v1:
time: 347 us; the launch traced here: 345 us
  waiting for transfers between devices  102 us (29%)
  matrix products  102 us (29%)
  starting transfers between devices  78.1 us (23%)
  local copies, waits for them, and re-layouts  22.7 us (7%)
  other arithmetic  15.4 us (4%)
  blocking collectives  13.9 us (4%)
  loops' own time  8.43 us (2%)
    ppermute x16, waiting for transfers between devices, halo_rows(): before = lax.ppermute(last, axis, up)  95.2 us
    dot_general x64, matrix products, product(): jnp.einsum('ij,jc->ic', matrix, operand, precision=lax.Precision.HIGHEST)  55.3 us
    dot_general x64, matrix products, product(): jnp.einsum('rbj,ji->rbi', operand, matrix, precision=lax.Precision.HIGH)  47.2 us
    ppermute x16, starting transfers between devices, halo_rows(): before = lax.ppermute(last, axis, up)  38 us
    ppermute x16, starting transfers between devices, halo_rows(): after = lax.ppermute(initial, axis, down)  33.4 us
    unnamed x1, blocking collectives  13.9 us
    another operation x1, loops' own time, body(): adjoint, terms = lax.fori_loop(0, layers, backward_step, (adjoint, terms))  6.98 us
  transfers between devices with their start and end apart: 34, of which 33 were waited for; matrix products, arithmetic and copies ran while one was open for 6% of the time, Pallas kernels for 0%

profile of v1, /device:TPU:2, one launch (start us, length us, event | category | flops | bytes accessed | tf_op | source)
XLA Modules:
  0.0 344.9 jit_solution(6944586890772344438)
XLA Ops:
  1.7 6.0 %all-to-all-start = ((bf16[8,1,16,2048]{3,2,1,0:T(8,128)(2,1)}), bf16[8,1,16,2048]{3,2,1,0:T(8,128)(2,1)S(1)}, u32[]{:S(2)}, u32[]{:S(2)}) async-start(bf16[8,1,16,2048]{3,2,1,0:T(8,128)(2,1)} %stack.123), calls=%async_computation | async-start | bytes 1048576 | tf_op jit(solution)/shard_map/all_to_all | solution.py:110
  13.0 13.9 %all-reduce.2 = s32[8]{0:T(128)S(1)} all-reduce(s32[8]{0:T(128)S(1)} %dynamic-update-slice), channel_id=1, replica_groups=mesh['depth'=8,'row'=32] {'depth'}, use_global_device_ids=true, to_apply=%add.2 | all-reduce | flops 8 | bytes 64
  27.6 3.7 %sine_bitcast_fusion = (f32[8,16,2048]{2,1,0:T(8,128)S(1)}, f32[8,16,2048]{2,1,0:T(8,128)S(1)}) fusion(bf16[8,1,16,2048]{3,2,1,0:T(8,128)(2,1)S(1)} %all-to-all-done), kind=kLoop, calls=%fused_computation.254 | loop fusion | flops 524288 | bytes 2621440 | tf_op jit(solution)/shard_map/sin | solution.py:121
  31.3 157.0 %while.38 = (s32[]{:T(128)}, f32[2,16,2048]{2,1,0:T(8,128)S(1)}, f32[8,2,16,2048]{3,2,1,0:T(8,128)}, s32[8]{0:T(128)S(1)}, f32[8,16,2048]{2,1,0:T(8,128)S(1)}, /*index=5*/f32[8,16,2048]{2,1,0:T(8,128)S(1)}, s32[]{:T(128)}) while((s32[]{:T(128)}, f32[2,16,2048]{2,1,0:T(8,128)S(1)}, f32[8,2,16,2048]{3,2,1,0:T(8,128)}, ...), condition=%wide.region_1.2_spmd.clone.clone, body=%wide.region_0.1_spmd.clone.clone.sunk | while | flops 273272320 | bytes 14237897 | solution.py:132
  31.4 4.6 %collective-permute-start = (f32[2,14,2048]{2,1,0:T(8,128)S(1)}, f32[2,14,2048]{2,1,0:T(8,128)S(1)}, u32[]{:S(2)}, u32[]{:S(2)}) collective-permute-start(f32[2,14,2048]{2,1,0:T(8,128)S(1)} %get-tuple-element.655), channel_id=1, source_target_pairs={{1,0},{2,1},{3,2},{4,3},{5,4},{6,5},{7,6},{8,7},{9,8},{10,9},{11,1... | collective-permute-start | bytes 688136 | tf_op jit(solution)/shard_map/while/body/eval_jaxpr/ppermute | solution.py:24
  36.1 1.9 collective-permute-start.1
  40.0 6.2 %collective-permute-done.1 = f32[2,14,2048]{2,1,0:T(8,128)S(1)} collective-permute-done((f32[2,14,2048]{2,1,0:T(8,128)S(1)}, f32[2,14,2048]{2,1,0:T(8,128)S(1)}, u32[]{:S(2)}, u32[]{:S(2)}) %collective-permute-start.1) | collective-permute-done | bytes 229408 | tf_op jit(solution)/shard_map/while/body/eval_jaxpr/ppermute | solution.py:23
  53.7 1.9 collective-permute-start
  55.6 2.4 collective-permute-start.1
  59.5 5.9 %collective-permute-done.1 = f32[2,14,2048]{2,1,0:T(8,128)S(1)} collective-permute-done((f32[2,14,2048]{2,1,0:T(8,128)S(1)}, f32[2,14,2048]{2,1,0:T(8,128)S(1)}, u32[]{:S(2)}, u32[]{:S(2)}) %collective-permute-start.1) | collective-permute-done | bytes 229408 | tf_op jit(solution)/shard_map/while/body/eval_jaxpr/ppermute | solution.py:23
  74.9 2.4 collective-permute-start.1
  78.8 5.9 %collective-permute-done.1 = f32[2,14,2048]{2,1,0:T(8,128)S(1)} collective-permute-done((f32[2,14,2048]{2,1,0:T(8,128)S(1)}, f32[2,14,2048]{2,1,0:T(8,128)S(1)}, u32[]{:S(2)}, u32[]{:S(2)}) %collective-permute-start.1) | collective-permute-done | bytes 229408 | tf_op jit(solution)/shard_map/while/body/eval_jaxpr/ppermute | solution.py:23
  94.1 2.4 collective-permute-start.1
  98.0 5.9 %collective-permute-done.1 = f32[2,14,2048]{2,1,0:T(8,128)S(1)} collective-permute-done((f32[2,14,2048]{2,1,0:T(8,128)S(1)}, f32[2,14,2048]{2,1,0:T(8,128)S(1)}, u32[]{:S(2)}, u32[]{:S(2)}) %collective-permute-start.1) | collective-permute-done | bytes 229408 | tf_op jit(solution)/shard_map/while/body/eval_jaxpr/ppermute | solution.py:23
  113.4 2.4 collective-permute-start.1
  117.3 5.9 %collective-permute-done.1 = f32[2,14,2048]{2,1,0:T(8,128)S(1)} collective-permute-done((f32[2,14,2048]{2,1,0:T(8,128)S(1)}, f32[2,14,2048]{2,1,0:T(8,128)S(1)}, u32[]{:S(2)}, u32[]{:S(2)}) %collective-permute-start.1) | collective-permute-done | bytes 229408 | tf_op jit(solution)/shard_map/while/body/eval_jaxpr/ppermute | solution.py:23
  132.7 2.4 collective-permute-start.1
  136.5 5.9 %collective-permute-done.1 = f32[2,14,2048]{2,1,0:T(8,128)S(1)} collective-permute-done((f32[2,14,2048]{2,1,0:T(8,128)S(1)}, f32[2,14,2048]{2,1,0:T(8,128)S(1)}, u32[]{:S(2)}, u32[]{:S(2)}) %collective-permute-start.1) | collective-permute-done | bytes 229408 | tf_op jit(solution)/shard_map/while/body/eval_jaxpr/ppermute | solution.py:23
  151.9 2.4 collective-permute-start.1
  155.8 5.9 %collective-permute-done.1 = f32[2,14,2048]{2,1,0:T(8,128)S(1)} collective-permute-done((f32[2,14,2048]{2,1,0:T(8,128)S(1)}, f32[2,14,2048]{2,1,0:T(8,128)S(1)}, u32[]{:S(2)}, u32[]{:S(2)}) %collective-permute-start.1) | collective-permute-done | bytes 229408 | tf_op jit(solution)/shard_map/while/body/eval_jaxpr/ppermute | solution.py:23
  171.2 2.4 collective-permute-start.1
  175.0 5.9 %collective-permute-done.1 = f32[2,14,2048]{2,1,0:T(8,128)S(1)} collective-permute-done((f32[2,14,2048]{2,1,0:T(8,128)S(1)}, f32[2,14,2048]{2,1,0:T(8,128)S(1)}, u32[]{:S(2)}, u32[]{:S(2)}) %collective-permute-start.1) | collective-permute-done | bytes 229408 | tf_op jit(solution)/shard_map/while/body/eval_jaxpr/ppermute | solution.py:23
  189.6 147.8 %while.39 = (s32[]{:T(128)}, f32[2,16,2048]{2,1,0:T(8,128)S(1)}, f32[8,16,2048]{2,1,0:T(8,128)}, f32[8,16,2048]{2,1,0:T(8,128)S(1)}, s32[8]{0:T(128)S(1)}, /*ind...) while((s32[]{:T(128)}, f32[2,16,2048]{2,1,0:T(8,128)S(1)}, ...), condition=%wide.region_3.4_spmd.clone.clone, body=%wide.region_2.3_spmd.clone.clone.sunk | while | flops 272724864 | bytes 14156587 | solution.py:149
  195.0 2.4 collective-permute-start.3
  198.9 5.9 %collective-permute-done.3 = f32[2,14,2048]{2,1,0:T(8,128)S(1)} collective-permute-done((f32[2,14,2048]{2,1,0:T(8,128)S(1)}, f32[2,14,2048]{2,1,0:T(8,128)S(1)}, u32[]{:S(2)}, u32[]{:S(2)}) %collective-permute-start.3) | collective-permute-done | bytes 229408 | tf_op jit(solution)/shard_map/while/body/eval_jaxpr/ppermute | solution.py:23
  205.9 2.0 fusion.246
  213.5 2.4 collective-permute-start.3
  217.3 5.9 %collective-permute-done.3 = f32[2,14,2048]{2,1,0:T(8,128)S(1)} collective-permute-done((f32[2,14,2048]{2,1,0:T(8,128)S(1)}, f32[2,14,2048]{2,1,0:T(8,128)S(1)}, u32[]{:S(2)}, u32[]{:S(2)}) %collective-permute-start.3) | collective-permute-done | bytes 229408 | tf_op jit(solution)/shard_map/while/body/eval_jaxpr/ppermute | solution.py:23
  224.4 2.0 fusion.246
  231.9 2.4 collective-permute-start.3
  235.8 5.9 %collective-permute-done.3 = f32[2,14,2048]{2,1,0:T(8,128)S(1)} collective-permute-done((f32[2,14,2048]{2,1,0:T(8,128)S(1)}, f32[2,14,2048]{2,1,0:T(8,128)S(1)}, u32[]{:S(2)}, u32[]{:S(2)}) %collective-permute-start.3) | collective-permute-done | bytes 229408 | tf_op jit(solution)/shard_map/while/body/eval_jaxpr/ppermute | solution.py:23
  242.9 2.0 fusion.246
  250.4 2.4 collective-permute-start.3
  254.3 5.9 %collective-permute-done.3 = f32[2,14,2048]{2,1,0:T(8,128)S(1)} collective-permute-done((f32[2,14,2048]{2,1,0:T(8,128)S(1)}, f32[2,14,2048]{2,1,0:T(8,128)S(1)}, u32[]{:S(2)}, u32[]{:S(2)}) %collective-permute-start.3) | collective-permute-done | bytes 229408 | tf_op jit(solution)/shard_map/while/body/eval_jaxpr/ppermute | solution.py:23
  261.4 2.0 fusion.246
  268.9 2.4 collective-permute-start.3
  272.8 5.9 %collective-permute-done.3 = f32[2,14,2048]{2,1,0:T(8,128)S(1)} collective-permute-done((f32[2,14,2048]{2,1,0:T(8,128)S(1)}, f32[2,14,2048]{2,1,0:T(8,128)S(1)}, u32[]{:S(2)}, u32[]{:S(2)}) %collective-permute-start.3) | collective-permute-done | bytes 229408 | tf_op jit(solution)/shard_map/while/body/eval_jaxpr/ppermute | solution.py:23
  279.9 2.0 fusion.246
  287.4 2.4 collective-permute-start.3
  291.2 5.9 %collective-permute-done.3 = f32[2,14,2048]{2,1,0:T(8,128)S(1)} collective-permute-done((f32[2,14,2048]{2,1,0:T(8,128)S(1)}, f32[2,14,2048]{2,1,0:T(8,128)S(1)}, u32[]{:S(2)}, u32[]{:S(2)}) %collective-permute-start.3) | collective-permute-done | bytes 229408 | tf_op jit(solution)/shard_map/while/body/eval_jaxpr/ppermute | solution.py:23
  298.3 2.0 fusion.246
  305.8 2.4 collective-permute-start.3
  309.7 5.9 %collective-permute-done.3 = f32[2,14,2048]{2,1,0:T(8,128)S(1)} collective-permute-done((f32[2,14,2048]{2,1,0:T(8,128)S(1)}, f32[2,14,2048]{2,1,0:T(8,128)S(1)}, u32[]{:S(2)}, u32[]{:S(2)}) %collective-permute-start.3) | collective-permute-done | bytes 229408 | tf_op jit(solution)/shard_map/while/body/eval_jaxpr/ppermute | solution.py:23
  316.8 2.0 fusion.246
  324.3 2.4 collective-permute-start.3
  328.2 5.9 %collective-permute-done.3 = f32[2,14,2048]{2,1,0:T(8,128)S(1)} collective-permute-done((f32[2,14,2048]{2,1,0:T(8,128)S(1)}, f32[2,14,2048]{2,1,0:T(8,128)S(1)}, u32[]{:S(2)}, u32[]{:S(2)}) %collective-permute-start.3) | collective-permute-done | bytes 229408 | tf_op jit(solution)/shard_map/while/body/eval_jaxpr/ppermute | solution.py:23
  335.3 2.0 fusion.246
  338.9 4.4 %collective-permute-done.4 = f32[1,16,2048]{2,1,0:T(8,128)S(1)} collective-permute-done((f32[1,16,2048]{2,1,0:T(8,128)S(1)}, f32[1,16,2048]{2,1,0:T(8,128)S(1)}, u32[]{:S(2)}, u32[]{:S(2)}) %collective-permute-start.4) | collective-permute-done | bytes 131104 | tf_op jit(solution)/shard_map/ppermute | solution.py:154
  (393 shorter events, 150.7 us)
Async XLA Ops:
  1.7 25.9 %all-to-all-start = ((bf16[8,1,16,2048]{3,2,1,0:T(8,128)(2,1)}), bf16[8,1,16,2048]{3,2,1,0:T(8,128)(2,1)S(1)}, u32[]{:S(2)}, u32[]{:S(2)}) async-start(bf16[8,1,16,2048]{3,2,1,0:T(8,128)(2,1)} %stack.123), calls=%async_computation | async-start | bytes 1048576 | tf_op jit(solution)/shard_map/all_to_all | solution.py:110
  31.3 157.1 %copy-start = (bf16[2,16,2048]{2,1,0:T(8,128)(2,1)S(1)}, bf16[2,16,2048]{2,1,0:T(8,128)(2,1)}, u32[]{:S(2)}) copy-start(bf16[2,16,2048]{2,1,0:T(8,128)(2,1)} %param.11) | copy-start | bytes 393220
  31.4 8.5 %collective-permute-start = (f32[2,14,2048]{2,1,0:T(8,128)S(1)}, f32[2,14,2048]{2,1,0:T(8,128)S(1)}, u32[]{:S(2)}, u32[]{:S(2)}) collective-permute-start(f32[2,14,2048]{2,1,0:T(8,128)S(1)} %get-tuple-element.655), channel_id=1, source_target_pairs={{1,0},{2,1},{3,2},{4,3},{5,4},{6,5},{7,6},{8,7},{9,8},{10,9},{11,1... | collective-permute-start | bytes 688136 | tf_op jit(solution)/shard_map/while/body/eval_jaxpr/ppermute | solution.py:24
  36.1 10.1 %collective-permute-start.1 = (f32[2,14,2048]{2,1,0:T(8,128)S(1)}, f32[2,14,2048]{2,1,0:T(8,128)S(1)}, u32[]{:S(2)}, u32[]{:S(2)}) collective-permute-start(f32[2,14,2048]{2,1,0:T(8,128)S(1)} %get-tuple-element.656), channel_id=1, source_target_pairs={{0,1},{1,2},{2,3},{3,4},{4,5},{5,6},{6,7},{7,8},{8,9},{9,10},{10,1... | collective-permute-start | bytes 688136 | tf_op jit(solution)/shard_map/while/body/eval_jaxpr/ppermute | solution.py:23
  53.7 5.8 %collective-permute-start = (f32[2,14,2048]{2,1,0:T(8,128)S(1)}, f32[2,14,2048]{2,1,0:T(8,128)S(1)}, u32[]{:S(2)}, u32[]{:S(2)}) collective-permute-start(f32[2,14,2048]{2,1,0:T(8,128)S(1)} %get-tuple-element.655), channel_id=1, source_target_pairs={{1,0},{2,1},{3,2},{4,3},{5,4},{6,5},{7,6},{8,7},{9,8},{10,9},{11,1... | collective-permute-start | bytes 688136 | tf_op jit(solution)/shard_map/while/body/eval_jaxpr/ppermute | solution.py:24
  55.6 9.8 %collective-permute-start.1 = (f32[2,14,2048]{2,1,0:T(8,128)S(1)}, f32[2,14,2048]{2,1,0:T(8,128)S(1)}, u32[]{:S(2)}, u32[]{:S(2)}) collective-permute-start(f32[2,14,2048]{2,1,0:T(8,128)S(1)} %get-tuple-element.656), channel_id=1, source_target_pairs={{0,1},{1,2},{2,3},{3,4},{4,5},{5,6},{6,7},{7,8},{8,9},{9,10},{10,1... | collective-permute-start | bytes 688136 | tf_op jit(solution)/shard_map/while/body/eval_jaxpr/ppermute | solution.py:23
  73.0 5.8 %collective-permute-start = (f32[2,14,2048]{2,1,0:T(8,128)S(1)}, f32[2,14,2048]{2,1,0:T(8,128)S(1)}, u32[]{:S(2)}, u32[]{:S(2)}) collective-permute-start(f32[2,14,2048]{2,1,0:T(8,128)S(1)} %get-tuple-element.655), channel_id=1, source_target_pairs={{1,0},{2,1},{3,2},{4,3},{5,4},{6,5},{7,6},{8,7},{9,8},{10,9},{11,1... | collective-permute-start | bytes 688136 | tf_op jit(solution)/shard_map/while/body/eval_jaxpr/ppermute | solution.py:24
  74.9 9.8 %collective-permute-start.1 = (f32[2,14,2048]{2,1,0:T(8,128)S(1)}, f32[2,14,2048]{2,1,0:T(8,128)S(1)}, u32[]{:S(2)}, u32[]{:S(2)}) collective-permute-start(f32[2,14,2048]{2,1,0:T(8,128)S(1)} %get-tuple-element.656), channel_id=1, source_target_pairs={{0,1},{1,2},{2,3},{3,4},{4,5},{5,6},{6,7},{7,8},{8,9},{9,10},{10,1... | collective-permute-start | bytes 688136 | tf_op jit(solution)/shard_map/while/body/eval_jaxpr/ppermute | solution.py:23
  92.2 5.8 %collective-permute-start = (f32[2,14,2048]{2,1,0:T(8,128)S(1)}, f32[2,14,2048]{2,1,0:T(8,128)S(1)}, u32[]{:S(2)}, u32[]{:S(2)}) collective-permute-start(f32[2,14,2048]{2,1,0:T(8,128)S(1)} %get-tuple-element.655), channel_id=1, source_target_pairs={{1,0},{2,1},{3,2},{4,3},{5,4},{6,5},{7,6},{8,7},{9,8},{10,9},{11,1... | collective-permute-start | bytes 688136 | tf_op jit(solution)/shard_map/while/body/eval_jaxpr/ppermute | solution.py:24
  94.1 9.8 %collective-permute-start.1 = (f32[2,14,2048]{2,1,0:T(8,128)S(1)}, f32[2,14,2048]{2,1,0:T(8,128)S(1)}, u32[]{:S(2)}, u32[]{:S(2)}) collective-permute-start(f32[2,14,2048]{2,1,0:T(8,128)S(1)} %get-tuple-element.656), channel_id=1, source_target_pairs={{0,1},{1,2},{2,3},{3,4},{4,5},{5,6},{6,7},{7,8},{8,9},{9,10},{10,1... | collective-permute-start | bytes 688136 | tf_op jit(solution)/shard_map/while/body/eval_jaxpr/ppermute | solution.py:23
  111.5 5.8 %collective-permute-start = (f32[2,14,2048]{2,1,0:T(8,128)S(1)}, f32[2,14,2048]{2,1,0:T(8,128)S(1)}, u32[]{:S(2)}, u32[]{:S(2)}) collective-permute-start(f32[2,14,2048]{2,1,0:T(8,128)S(1)} %get-tuple-element.655), channel_id=1, source_target_pairs={{1,0},{2,1},{3,2},{4,3},{5,4},{6,5},{7,6},{8,7},{9,8},{10,9},{11,1... | collective-permute-start | bytes 688136 | tf_op jit(solution)/shard_map/while/body/eval_jaxpr/ppermute | solution.py:24
  113.4 9.8 %collective-permute-start.1 = (f32[2,14,2048]{2,1,0:T(8,128)S(1)}, f32[2,14,2048]{2,1,0:T(8,128)S(1)}, u32[]{:S(2)}, u32[]{:S(2)}) collective-permute-start(f32[2,14,2048]{2,1,0:T(8,128)S(1)} %get-tuple-element.656), channel_id=1, source_target_pairs={{0,1},{1,2},{2,3},{3,4},{4,5},{5,6},{6,7},{7,8},{8,9},{9,10},{10,1... | collective-permute-start | bytes 688136 | tf_op jit(solution)/shard_map/while/body/eval_jaxpr/ppermute | solution.py:23
  130.7 5.8 %collective-permute-start = (f32[2,14,2048]{2,1,0:T(8,128)S(1)}, f32[2,14,2048]{2,1,0:T(8,128)S(1)}, u32[]{:S(2)}, u32[]{:S(2)}) collective-permute-start(f32[2,14,2048]{2,1,0:T(8,128)S(1)} %get-tuple-element.655), channel_id=1, source_target_pairs={{1,0},{2,1},{3,2},{4,3},{5,4},{6,5},{7,6},{8,7},{9,8},{10,9},{11,1... | collective-permute-start | bytes 688136 | tf_op jit(solution)/shard_map/while/body/eval_jaxpr/ppermute | solution.py:24
  132.7 9.8 %collective-permute-start.1 = (f32[2,14,2048]{2,1,0:T(8,128)S(1)}, f32[2,14,2048]{2,1,0:T(8,128)S(1)}, u32[]{:S(2)}, u32[]{:S(2)}) collective-permute-start(f32[2,14,2048]{2,1,0:T(8,128)S(1)} %get-tuple-element.656), channel_id=1, source_target_pairs={{0,1},{1,2},{2,3},{3,4},{4,5},{5,6},{6,7},{7,8},{8,9},{9,10},{10,1... | collective-permute-start | bytes 688136 | tf_op jit(solution)/shard_map/while/body/eval_jaxpr/ppermute | solution.py:23
  150.0 5.8 %collective-permute-start = (f32[2,14,2048]{2,1,0:T(8,128)S(1)}, f32[2,14,2048]{2,1,0:T(8,128)S(1)}, u32[]{:S(2)}, u32[]{:S(2)}) collective-permute-start(f32[2,14,2048]{2,1,0:T(8,128)S(1)} %get-tuple-element.655), channel_id=1, source_target_pairs={{1,0},{2,1},{3,2},{4,3},{5,4},{6,5},{7,6},{8,7},{9,8},{10,9},{11,1... | collective-permute-start | bytes 688136 | tf_op jit(solution)/shard_map/while/body/eval_jaxpr/ppermute | solution.py:24
  151.9 9.8 %collective-permute-start.1 = (f32[2,14,2048]{2,1,0:T(8,128)S(1)}, f32[2,14,2048]{2,1,0:T(8,128)S(1)}, u32[]{:S(2)}, u32[]{:S(2)}) collective-permute-start(f32[2,14,2048]{2,1,0:T(8,128)S(1)} %get-tuple-element.656), channel_id=1, source_target_pairs={{0,1},{1,2},{2,3},{3,4},{4,5},{5,6},{6,7},{7,8},{8,9},{9,10},{10,1... | collective-permute-start | bytes 688136 | tf_op jit(solution)/shard_map/while/body/eval_jaxpr/ppermute | solution.py:23
  169.2 5.8 %collective-permute-start = (f32[2,14,2048]{2,1,0:T(8,128)S(1)}, f32[2,14,2048]{2,1,0:T(8,128)S(1)}, u32[]{:S(2)}, u32[]{:S(2)}) collective-permute-start(f32[2,14,2048]{2,1,0:T(8,128)S(1)} %get-tuple-element.655), channel_id=1, source_target_pairs={{1,0},{2,1},{3,2},{4,3},{5,4},{6,5},{7,6},{8,7},{9,8},{10,9},{11,1... | collective-permute-start | bytes 688136 | tf_op jit(solution)/shard_map/while/body/eval_jaxpr/ppermute | solution.py:24
  171.2 9.8 %collective-permute-start.1 = (f32[2,14,2048]{2,1,0:T(8,128)S(1)}, f32[2,14,2048]{2,1,0:T(8,128)S(1)}, u32[]{:S(2)}, u32[]{:S(2)}) collective-permute-start(f32[2,14,2048]{2,1,0:T(8,128)S(1)} %get-tuple-element.656), channel_id=1, source_target_pairs={{0,1},{1,2},{2,3},{3,4},{4,5},{5,6},{6,7},{7,8},{8,9},{9,10},{10,1... | collective-permute-start | bytes 688136 | tf_op jit(solution)/shard_map/while/body/eval_jaxpr/ppermute | solution.py:23
  193.1 5.8 %collective-permute-start.2 = (f32[2,14,2048]{2,1,0:T(8,128)S(1)}, f32[2,14,2048]{2,1,0:T(8,128)S(1)}, u32[]{:S(2)}, u32[]{:S(2)}) collective-permute-start(f32[2,14,2048]{2,1,0:T(8,128)S(1)} %get-tuple-element.668), channel_id=1, source_target_pairs={{1,0},{2,1},{3,2},{4,3},{5,4},{6,5},{7,6},{8,7},{9,8},{10,9},{11,1... | collective-permute-start | bytes 688136 | tf_op jit(solution)/shard_map/while/body/eval_jaxpr/ppermute | solution.py:24
  195.0 9.8 %collective-permute-start.3 = (f32[2,14,2048]{2,1,0:T(8,128)S(1)}, f32[2,14,2048]{2,1,0:T(8,128)S(1)}, u32[]{:S(2)}, u32[]{:S(2)}) collective-permute-start(f32[2,14,2048]{2,1,0:T(8,128)S(1)} %get-tuple-element.669), channel_id=1, source_target_pairs={{0,1},{1,2},{2,3},{3,4},{4,5},{5,6},{6,7},{7,8},{8,9},{9,10},{10,1... | collective-permute-start | bytes 688136 | tf_op jit(solution)/shard_map/while/body/eval_jaxpr/ppermute | solution.py:23
  211.5 5.8 %collective-permute-start.2 = (f32[2,14,2048]{2,1,0:T(8,128)S(1)}, f32[2,14,2048]{2,1,0:T(8,128)S(1)}, u32[]{:S(2)}, u32[]{:S(2)}) collective-permute-start(f32[2,14,2048]{2,1,0:T(8,128)S(1)} %get-tuple-element.668), channel_id=1, source_target_pairs={{1,0},{2,1},{3,2},{4,3},{5,4},{6,5},{7,6},{8,7},{9,8},{10,9},{11,1... | collective-permute-start | bytes 688136 | tf_op jit(solution)/shard_map/while/body/eval_jaxpr/ppermute | solution.py:24
  213.5 9.8 %collective-permute-start.3 = (f32[2,14,2048]{2,1,0:T(8,128)S(1)}, f32[2,14,2048]{2,1,0:T(8,128)S(1)}, u32[]{:S(2)}, u32[]{:S(2)}) collective-permute-start(f32[2,14,2048]{2,1,0:T(8,128)S(1)} %get-tuple-element.669), channel_id=1, source_target_pairs={{0,1},{1,2},{2,3},{3,4},{4,5},{5,6},{6,7},{7,8},{8,9},{9,10},{10,1... | collective-permute-start | bytes 688136 | tf_op jit(solution)/shard_map/while/body/eval_jaxpr/ppermute | solution.py:23
  230.0 5.8 %collective-permute-start.2 = (f32[2,14,2048]{2,1,0:T(8,128)S(1)}, f32[2,14,2048]{2,1,0:T(8,128)S(1)}, u32[]{:S(2)}, u32[]{:S(2)}) collective-permute-start(f32[2,14,2048]{2,1,0:T(8,128)S(1)} %get-tuple-element.668), channel_id=1, source_target_pairs={{1,0},{2,1},{3,2},{4,3},{5,4},{6,5},{7,6},{8,7},{9,8},{10,9},{11,1... | collective-permute-start | bytes 688136 | tf_op jit(solution)/shard_map/while/body/eval_jaxpr/ppermute | solution.py:24
  231.9 9.8 %collective-permute-start.3 = (f32[2,14,2048]{2,1,0:T(8,128)S(1)}, f32[2,14,2048]{2,1,0:T(8,128)S(1)}, u32[]{:S(2)}, u32[]{:S(2)}) collective-permute-start(f32[2,14,2048]{2,1,0:T(8,128)S(1)} %get-tuple-element.669), channel_id=1, source_target_pairs={{0,1},{1,2},{2,3},{3,4},{4,5},{5,6},{6,7},{7,8},{8,9},{9,10},{10,1... | collective-permute-start | bytes 688136 | tf_op jit(solution)/shard_map/while/body/eval_jaxpr/ppermute | solution.py:23
  248.5 5.8 %collective-permute-start.2 = (f32[2,14,2048]{2,1,0:T(8,128)S(1)}, f32[2,14,2048]{2,1,0:T(8,128)S(1)}, u32[]{:S(2)}, u32[]{:S(2)}) collective-permute-start(f32[2,14,2048]{2,1,0:T(8,128)S(1)} %get-tuple-element.668), channel_id=1, source_target_pairs={{1,0},{2,1},{3,2},{4,3},{5,4},{6,5},{7,6},{8,7},{9,8},{10,9},{11,1... | collective-permute-start | bytes 688136 | tf_op jit(solution)/shard_map/while/body/eval_jaxpr/ppermute | solution.py:24
  250.4 9.8 %collective-permute-start.3 = (f32[2,14,2048]{2,1,0:T(8,128)S(1)}, f32[2,14,2048]{2,1,0:T(8,128)S(1)}, u32[]{:S(2)}, u32[]{:S(2)}) collective-permute-start(f32[2,14,2048]{2,1,0:T(8,128)S(1)} %get-tuple-element.669), channel_id=1, source_target_pairs={{0,1},{1,2},{2,3},{3,4},{4,5},{5,6},{6,7},{7,8},{8,9},{9,10},{10,1... | collective-permute-start | bytes 688136 | tf_op jit(solution)/shard_map/while/body/eval_jaxpr/ppermute | solution.py:23
  267.0 5.8 %collective-permute-start.2 = (f32[2,14,2048]{2,1,0:T(8,128)S(1)}, f32[2,14,2048]{2,1,0:T(8,128)S(1)}, u32[]{:S(2)}, u32[]{:S(2)}) collective-permute-start(f32[2,14,2048]{2,1,0:T(8,128)S(1)} %get-tuple-element.668), channel_id=1, source_target_pairs={{1,0},{2,1},{3,2},{4,3},{5,4},{6,5},{7,6},{8,7},{9,8},{10,9},{11,1... | collective-permute-start | bytes 688136 | tf_op jit(solution)/shard_map/while/body/eval_jaxpr/ppermute | solution.py:24
  268.9 9.8 %collective-permute-start.3 = (f32[2,14,2048]{2,1,0:T(8,128)S(1)}, f32[2,14,2048]{2,1,0:T(8,128)S(1)}, u32[]{:S(2)}, u32[]{:S(2)}) collective-permute-start(f32[2,14,2048]{2,1,0:T(8,128)S(1)} %get-tuple-element.669), channel_id=1, source_target_pairs={{0,1},{1,2},{2,3},{3,4},{4,5},{5,6},{6,7},{7,8},{8,9},{9,10},{10,1... | collective-permute-start | bytes 688136 | tf_op jit(solution)/shard_map/while/body/eval_jaxpr/ppermute | solution.py:23
  285.4 5.8 %collective-permute-start.2 = (f32[2,14,2048]{2,1,0:T(8,128)S(1)}, f32[2,14,2048]{2,1,0:T(8,128)S(1)}, u32[]{:S(2)}, u32[]{:S(2)}) collective-permute-start(f32[2,14,2048]{2,1,0:T(8,128)S(1)} %get-tuple-element.668), channel_id=1, source_target_pairs={{1,0},{2,1},{3,2},{4,3},{5,4},{6,5},{7,6},{8,7},{9,8},{10,9},{11,1... | collective-permute-start | bytes 688136 | tf_op jit(solution)/shard_map/while/body/eval_jaxpr/ppermute | solution.py:24
  287.4 9.8 %collective-permute-start.3 = (f32[2,14,2048]{2,1,0:T(8,128)S(1)}, f32[2,14,2048]{2,1,0:T(8,128)S(1)}, u32[]{:S(2)}, u32[]{:S(2)}) collective-permute-start(f32[2,14,2048]{2,1,0:T(8,128)S(1)} %get-tuple-element.669), channel_id=1, source_target_pairs={{0,1},{1,2},{2,3},{3,4},{4,5},{5,6},{6,7},{7,8},{8,9},{9,10},{10,1... | collective-permute-start | bytes 688136 | tf_op jit(solution)/shard_map/while/body/eval_jaxpr/ppermute | solution.py:23
  303.9 5.8 %collective-permute-start.2 = (f32[2,14,2048]{2,1,0:T(8,128)S(1)}, f32[2,14,2048]{2,1,0:T(8,128)S(1)}, u32[]{:S(2)}, u32[]{:S(2)}) collective-permute-start(f32[2,14,2048]{2,1,0:T(8,128)S(1)} %get-tuple-element.668), channel_id=1, source_target_pairs={{1,0},{2,1},{3,2},{4,3},{5,4},{6,5},{7,6},{8,7},{9,8},{10,9},{11,1... | collective-permute-start | bytes 688136 | tf_op jit(solution)/shard_map/while/body/eval_jaxpr/ppermute | solution.py:24
  305.8 9.8 %collective-permute-start.3 = (f32[2,14,2048]{2,1,0:T(8,128)S(1)}, f32[2,14,2048]{2,1,0:T(8,128)S(1)}, u32[]{:S(2)}, u32[]{:S(2)}) collective-permute-start(f32[2,14,2048]{2,1,0:T(8,128)S(1)} %get-tuple-element.669), channel_id=1, source_target_pairs={{0,1},{1,2},{2,3},{3,4},{4,5},{5,6},{6,7},{7,8},{8,9},{9,10},{10,1... | collective-permute-start | bytes 688136 | tf_op jit(solution)/shard_map/while/body/eval_jaxpr/ppermute | solution.py:23
  322.4 5.8 %collective-permute-start.2 = (f32[2,14,2048]{2,1,0:T(8,128)S(1)}, f32[2,14,2048]{2,1,0:T(8,128)S(1)}, u32[]{:S(2)}, u32[]{:S(2)}) collective-permute-start(f32[2,14,2048]{2,1,0:T(8,128)S(1)} %get-tuple-element.668), channel_id=1, source_target_pairs={{1,0},{2,1},{3,2},{4,3},{5,4},{6,5},{7,6},{8,7},{9,8},{10,9},{11,1... | collective-permute-start | bytes 688136 | tf_op jit(solution)/shard_map/while/body/eval_jaxpr/ppermute | solution.py:24
  324.3 9.8 %collective-permute-start.3 = (f32[2,14,2048]{2,1,0:T(8,128)S(1)}, f32[2,14,2048]{2,1,0:T(8,128)S(1)}, u32[]{:S(2)}, u32[]{:S(2)}) collective-permute-start(f32[2,14,2048]{2,1,0:T(8,128)S(1)} %get-tuple-element.669), channel_id=1, source_target_pairs={{0,1},{1,2},{2,3},{3,4},{4,5},{5,6},{6,7},{7,8},{8,9},{9,10},{10,1... | collective-permute-start | bytes 688136 | tf_op jit(solution)/shard_map/while/body/eval_jaxpr/ppermute | solution.py:23
  338.3 5.1 %collective-permute-start.4 = (f32[1,16,2048]{2,1,0:T(8,128)S(1)}, f32[1,16,2048]{2,1,0:T(8,128)S(1)}, u32[]{:S(2)}, u32[]{:S(2)}) collective-permute-start(f32[1,16,2048]{2,1,0:T(8,128)S(1)} %constant_dynamic-slice_fusion), channel_id=1, source_target_pairs={{0,32},{32,0},{64,96},{96,64},{128,160},{160,128},{192,224},{224,1... | collective-permute-start | bytes 393224 | tf_op jit(solution)/shard_map/ppermute | solution.py:154
